TPU v7x, 512 devices: a whole 4x4x16 slice. The times are simulated.
512 devices in a mesh: grp: 32 (over y, x, core), tp: 16 (over z).
Axes of the slice: x: 4, y: 4, z: 16, core: 2. Of those that a mesh axis runs over, the one named last changes fastest.
Arguments:
- trainer_increment: float32 [1024, 128, 128], P(('tp', 'grp')), may hold values from -0.3125 to 0.3125
- trainer_residual: float32 [1024, 128, 128], P(('tp', 'grp')), may hold values from -0.3125 to 0.3125
- partition_tile_indices: int32 [512, 2], P(('tp', 'grp')), may hold values from 0 to 1, as said below
- retained_tallies: int32 [512], P(('tp', 'grp')), may hold values from 0 to 2, as said below
- projection_parameters: bfloat16 [8192, 2048], P('tp'), may hold values from -0.0625 to 0.0625
- normalized_activations: bfloat16 [4, 32, 8192], P(None, 'grp', 'tp'), may hold values from -6 to 6
- rotated_questions: bfloat16 [4, 32, 8192], P(None, 'grp'), may hold values from -256 to 256
- stored_attention_memory: bfloat16 [32, 8192, 2048], P('grp', 'tp'), may hold values from -6 to 6
- memory_fill_lengths: int32 [32], P('grp'), may hold values from 2 to 8192, as said below
Outputs:
- new_error: float32 [1024, 128, 128], P(('tp', 'grp'))
- new_kv: bfloat16 [4, 32, 2048], P(None, 'grp', 'tp')
- attention: bfloat16 [4, 32, 8192], P(None, 'grp', 'tp')
Inputs may be any that keep to these rules, and one draw needn't show every extreme that they name: `partition_tile_indices`: each row lists the local block numbers of one shard, each once; only its first retained_tallies entries name surviving blocks. `retained_tallies`: some shard lists all 2 of its blocks in every draw. Row r's valid cache positions are 0 to memory_fill_lengths[r] - 1; some row has all 8192 in every draw.
All inputs are finite; a program needn't handle non-finite values.
Results may differ from a plain program's by a relative error of at most 0.02.
Values may be sent and summed in bfloat16 or wider, within the bound.
A program may use at most 64 MiB of HBM per device.

v0:
```python
import math
import jax
import jax.numpy as jnp
from jax import lax
from jax.sharding import PartitionSpec as P

HD = 128
BLK = 128
NEG = -1e30


def merged(array, axis, combine):
    everything = jax.tree.map(lambda part: lax.all_gather(part, axis), array)
    initial = jax.tree.map(lambda part: part[0], everything)

    def step(k, so_far):
        return combine(so_far, jax.tree.map(lambda part: part[k], everything))

    return lax.fori_loop(1, lax.axis_size(axis), step, initial)


def retained_tiles(partition_tile_indices, retained_tallies):
    slots = partition_tile_indices.shape[1]
    sorting_permutation = jnp.arange(slots, dtype=jnp.int32)
    enumerated_tiles = sorting_permutation[None, :] < retained_tallies[:, None]
    hits = (
        partition_tile_indices[:, :, None] == sorting_permutation[None, None, :]
    ) & enumerated_tiles[:, :, None]
    return jnp.any(hits, axis=1)


def combine(first, second):
    top_a, total_a, blended_first = first
    top_b, total_b, mixed_b = second
    top = jnp.maximum(top_a, top_b)
    scale_a = jnp.exp(top_a - top)
    scale_b = jnp.exp(top_b - top)
    total = total_a * scale_a + total_b * scale_b
    mixed = blended_first * scale_a[..., None] + mixed_b * scale_b[..., None]
    return (top, total, mixed)


def cache_partial(rotated_questions, stored_attention_memory, memory_fill_lengths, first):
    steps, rows, width = rotated_questions.shape
    span = stored_attention_memory.shape[1]
    heads_kv = stored_attention_memory.shape[2] // (2 * HD)
    group = width // HD // heads_kv
    scale = 1.0 / math.sqrt(HD)
    query = rotated_questions.reshape(steps, rows, heads_kv, group, HD)
    cache_rows_held = stored_attention_memory.reshape(rows, span, heads_kv, 2, HD)
    scores = (
        jnp.einsum(
            "srhgd,rphd->srhgp",
            query,
            cache_rows_held[:, :, :, 0],
            preferred_element_type=jnp.float32,
        )
        * scale
    )
    position = first + jnp.arange(span, dtype=jnp.int32)
    valid = (position[None, :] < memory_fill_lengths[:, None])[None, :, None, None, :]
    scores = jnp.where(valid, scores, NEG)
    top = jnp.max(scores, axis=-1)
    probs = jnp.where(valid, jnp.exp(scores - top[..., None]), 0.0)
    total = jnp.sum(probs, axis=-1)
    values = cache_rows_held[:, :, :, 1].astype(jnp.float32)
    mixed = jnp.einsum("srhgp,rphd->srhgd", probs, values, precision=lax.Precision.HIGHEST)
    heads = heads_kv * group
    return (
        top.reshape(steps, rows, heads),
        total.reshape(steps, rows, heads),
        mixed.reshape(steps, rows, heads, HD),
    )


def body(
    trainer_increment,
    trainer_residual,
    partition_tile_indices,
    retained_tallies,
    projection_parameters,
    normalized_activations,
    rotated_questions,
    stored_attention_memory,
    memory_fill_lengths,
):
    summed = trainer_increment + trainer_residual
    retain_markers = retained_tiles(partition_tile_indices, retained_tallies).reshape(-1)
    sent = jnp.where(
        retain_markers[:, None, None], summed.astype(jnp.bfloat16), jnp.zeros((), jnp.bfloat16)
    )
    new_error = summed - sent.astype(jnp.float32)
    blocks = lax.all_gather(sent, "grp", axis=0, tiled=True)
    local_feats, kvw = projection_parameters.shape
    update = (
        blocks.reshape(local_feats // BLK, kvw // BLK, BLK, BLK)
        .transpose(0, 2, 1, 3)
        .reshape(local_feats, kvw)
    )
    patched = (projection_parameters.astype(jnp.float32) + update.astype(jnp.float32)).astype(
        jnp.bfloat16
    )
    steps, local_rows, width = normalized_activations.shape
    partial_kv = jnp.dot(
        normalized_activations.reshape(steps * local_rows, width),
        patched,
        preferred_element_type=jnp.float32,
    )
    ranks = lax.axis_size("tp")
    rank = lax.axis_index("tp")
    columns = kvw // ranks
    kv_full = lax.psum(partial_kv, "tp").astype(jnp.bfloat16)
    kv_own = lax.dynamic_slice_in_dim(kv_full, rank * columns, columns, 1)
    new_kv = kv_own.reshape(steps, local_rows, columns)
    span = stored_attention_memory.shape[1]
    top, total, mixed = cache_partial(
        rotated_questions, stored_attention_memory, memory_fill_lengths, rank * span
    )
    heads = top.shape[2]
    own = heads // ranks
    top, total, mixed = merged((top, total, mixed), "tp", combine)
    top = lax.dynamic_slice_in_dim(top, rank * own, own, 2)
    total = lax.dynamic_slice_in_dim(total, rank * own, own, 2)
    mixed = lax.dynamic_slice_in_dim(mixed, rank * own, own, 2)
    heads_kv = kvw // (2 * HD)
    group = heads // heads_kv
    scale = 1.0 / math.sqrt(HD)
    fresh = kv_full.reshape(steps, local_rows, heads_kv, 2, HD)
    head_ids = (rank * own + jnp.arange(own, dtype=jnp.int32)) // group
    fresh = jnp.take(fresh, head_ids, axis=2)
    query = lax.dynamic_slice_in_dim(rotated_questions, rank * own * HD, own * HD, 2).reshape(
        steps, local_rows, own, HD
    )
    scores = (
        jnp.einsum("srjd,urjd->srju", query, fresh[:, :, :, 0], preferred_element_type=jnp.float32)
        * scale
    )
    step_ids = jnp.arange(steps, dtype=jnp.int32)
    causal = (step_ids[None, :] <= step_ids[:, None])[:, None, None, :]
    scores = jnp.where(causal, scores, NEG)
    peak = jnp.maximum(top, jnp.max(scores, axis=-1))
    probs = jnp.where(causal, jnp.exp(scores - peak[..., None]), 0.0)
    carried = jnp.exp(top - peak)
    denom = total * carried + jnp.sum(probs, axis=-1)
    values = fresh[:, :, :, 1].astype(jnp.float32)
    numer = mixed * carried[..., None] + jnp.einsum(
        "srju,urjd->srjd", probs, values, precision=lax.Precision.HIGHEST
    )
    attention = (numer / denom[..., None]).reshape(steps, local_rows, own * HD).astype(jnp.bfloat16)
    return (new_error, new_kv, attention)


def solution(mesh):
    placed = (
        P(("tp", "grp"), None, None),
        P(("tp", "grp"), None, None),
        P(("tp", "grp"), None),
        P(("tp", "grp")),
        P("tp", None),
        P(None, "grp", "tp"),
        P(None, "grp", None),
        P("grp", "tp", None),
        P("grp"),
    )
    return jax.shard_map(
        body,
        mesh=mesh,
        in_specs=placed,
        out_specs=(P(("tp", "grp"), None, None), P(None, "grp", "tp"), P(None, "grp", "tp")),
        check_vma=False,
    )
```

profile of v0, /device:TPU:2, one launch (start us, length us, event | category | flops | bytes accessed | tf_op | source)
XLA Modules:
  0.0 221.9 jit_solution(10214104289567611357)
XLA Ops:
  7.2 0.0 copy-start
  7.2 0.0 all-gather.5.cloned.1.call-start
  7.2 0.0 copy-start.4
  7.2 2.9 %copy.91 = bf16[1,512,2048]{1,2,0:T(8,128)(2,1)S(1)} copy(bf16[1,512,2048]{2,1,0:T(8,128)(2,1)} %param.18) | data formatting | bytes 4194304 | tf_op args[7]
  10.8 0.0 copy-done.4
  10.8 0.0 copy-start.5
  10.8 0.0 copy-start.2
  10.8 0.0 copy-start.3
  10.9 0.4 fusion.34
  11.2 1.1 convolution_bitcast_fusion.1
  12.4 0.7 copy.134
  13.0 0.0 all-gather.5.cloned.1.call-update
  13.1 0.0 all-gather.3.cloned.1.call-start
  13.8 0.0 copy-done.5
  13.8 0.1 and_reduce_fusion
  13.9 0.0 copy-done.2
  13.9 0.0 copy-done.3
  13.9 0.7 convert_select_fusion
  14.6 0.0 all-gather.3.cloned.1.call-update
  14.6 0.7 convert_subtract_fusion
  15.3 0.2 fusion.13
  15.6 0.1 all_gather_reshape.9
  15.7 35.6 %all_gather.13 = f32[16,4,1,64]{3,1,2,0:T(4,128)S(1)} all-gather(f32[1,4,1,64]{3,1,2,0:T(4,128)S(1)} %all_gather_reshape.9), channel_id=1, replica_groups=mesh['grp'=32,'tp'=16] {'tp'}, dimensions={0}, use_global_device_ids=true | all-gather | bytes 17408 | tf_op jit(solution)/shard_map/all_gather | solution.py:13
  51.3 0.1 all_gather_reshape.10
  51.4 26.1 %all_gather.14 = f32[16,4,1,64]{3,1,2,0:T(4,128)S(1)} all-gather(f32[1,4,1,64]{3,1,2,0:T(4,128)S(1)} %all_gather_reshape.10), channel_id=1, replica_groups=mesh['grp'=32,'tp'=16] {'tp'}, dimensions={0}, use_global_device_ids=true | all-gather | bytes 17408 | tf_op jit(solution)/shard_map/all_gather | solution.py:13
  77.5 13.1 %all-gather.5.cloned.1.call-done = f32[16,4,1,64,128]{4,3,2,1,0:T(8,128)} async-done(((f32[1,4,1,64,128]{4,3,2,1,0:T(8,128)}), f32[16,4,1,64,128]{4,3,2,1,0:T(8,128)}) %all-gather.5.cloned.1.call-update) | async-done | bytes 2097168 | tf_op jit(solution)/shard_map/all_gather | solution.py:13
  90.5 0.9 slice_bitcast_fusion.4
  91.5 17.1 %while.19 = (s32[]{:T(128)}, f32[4,1,64]{2,1,0:T(1,128)S(1)}, f32[4,1,64]{2,1,0:T(1,128)S(1)}, f32[4,1,64,128]{3,2,1,0:T(8,128)S(1)}, f32[16,4,1,64]{3,1,2,0:T(4...) while((s32[]{:T(128)}, f32[4,1,64]{2,1,0:T(1,128)S(1)}, ...), condition=%wide.region_5.6_spmd, body=%wide.region_4.5_spmd.sunk | while | flops 99845 | bytes 407703 | solution.py:19
  91.5 1.1 fusion.37
  92.7 1.1 fusion.37
  93.8 1.1 fusion.37
  94.9 1.1 fusion.37
  96.1 1.1 fusion.37
  97.2 1.1 fusion.37
  98.4 1.1 fusion.37
  99.5 1.1 fusion.37
  100.6 1.1 fusion.37
  101.8 1.1 fusion.37
  102.9 1.1 fusion.37
  104.1 1.1 fusion.37
  105.2 1.1 fusion.37
  106.3 1.1 fusion.37
  107.5 1.1 fusion.37
  108.6 0.1 copy.103
  108.7 40.8 %all-gather.3.cloned.1.call-done = bf16[64,128,128]{2,1,0:T(8,128)(2,1)} async-done(((bf16[2,128,128]{2,1,0:T(8,128)(2,1)}), bf16[64,128,128]{2,1,0:T(8,128)(2,1)}) %all-gather.3.cloned.1.call-update) | async-done | bytes 2097168 | tf_op jit(solution)/shard_map/all_gather | solution.py:93
  149.5 2.1 convert_bitcast_fusion
  151.6 0.0 copy-start.1
  151.6 2.4 %copy.90 = f32[4,128,16,128]{3,2,1,0:T(8,128)S(1)} copy(f32[4,128,16,128]{3,1,2,0:T(8,128)S(1)} %convert_bitcast_fusion) | data formatting | bytes 8388608 | tf_op jit(solution)/shard_map/convert_element_type | solution.py:100
  154.0 0.0 copy-done
  154.0 0.0 copy-done.1
  154.1 1.3 convolution_bitcast_fusion
  155.4 56.9 %psum.7 = bf16[4,2048]{1,0:T(4,128)(2,1)S(1)} all-reduce(f32[4,2048]{1,0:T(4,128)S(1)} %convolution_bitcast_fusion), channel_id=1, replica_groups=mesh['grp'=32,'tp'=16] {'tp'}, use_global_device_ids=true, to_apply=%region_1.2 | all-reduce | flops 8192 | bytes 49152 | tf_op jit(solution)/shard_map/psum | solution.py:112
  212.3 0.6 fusion.29
  212.8 0.6 gather_fusion
  213.4 0.1 bitcast_select_fusion
  213.5 0.1 fusion.35
  213.6 0.1 copy.107
  213.7 0.1 fusion.27
  213.8 0.1 copy.109
  213.9 0.1 copy.113
  214.0 0.1 fusion.31
  214.1 0.1 copy.114
  214.2 0.1 copy.108
  214.3 0.8 fusion.10
  (41 shorter events, 0.6 us)
Async XLA Ops:
  7.2 146.9 %copy-start = (bf16[4,1,512]{2,0,1:T(4,128)(2,1)S(1)}, bf16[4,1,512]{2,0,1:T(4,128)(2,1)}, u32[]{:S(2)}) copy-start(bf16[4,1,512]{2,0,1:T(4,128)(2,1)} %param.16) | copy-start | bytes 12292
  7.2 83.4 %all-gather.5.cloned.1.call-start = ((), (), s32[]{:S(2)}) async-start(), calls=%async_computation.1 | async-start | bytes 2228224 | tf_op jit(solution)/shard_map/all_gather | solution.py:13
  7.2 3.6 %copy-start.4 = (bf16[4,1,8192]{2,0,1:T(4,128)(2,1)S(1)}, bf16[4,1,8192]{2,0,1:T(4,128)(2,1)}, u32[]{:S(2)}) copy-start(bf16[4,1,8192]{2,0,1:T(4,128)(2,1)} %param.17) | copy-start | bytes 196612
  10.8 3.0 %copy-start.5 = (s32[1,2]{1,0:T(1,128)S(1)}, s32[1,2]{1,0:T(1,128)}, u32[]{:S(2)}) copy-start(s32[1,2]{1,0:T(1,128)} %param.13) | copy-start | bytes 28
  10.8 3.0 %copy-start.2 = (f32[2,128,128]{2,1,0:T(8,128)S(1)}, f32[2,128,128]{2,1,0:T(8,128)}, u32[]{:S(2)}) copy-start(f32[2,128,128]{2,1,0:T(8,128)} %param.11) | copy-start | bytes 393220
  10.8 3.0 %copy-start.3 = (f32[2,128,128]{2,1,0:T(8,128)S(1)}, f32[2,128,128]{2,1,0:T(8,128)}, u32[]{:S(2)}) copy-start(f32[2,128,128]{2,1,0:T(8,128)} %param.12) | copy-start | bytes 393220
  13.1 136.4 %all-gather.3.cloned.1.call-start = ((), (), s32[]{:S(2)}) async-start(), calls=%async_computation | async-start | bytes 2162688 | tf_op jit(solution)/shard_map/all_gather | solution.py:93
  151.6 2.5 %copy-start.1 = (bf16[512,2048]{1,0:T(8,128)(2,1)S(1)}, bf16[512,2048]{1,0:T(8,128)(2,1)}, u32[]{:S(2)}) copy-start(bf16[512,2048]{1,0:T(8,128)(2,1)} %param.15) | copy-start | bytes 6291460
Sparse Core Ops, SparseCore 0:
  13.2 77.3 all-gather.4
  93.7 55.7 all-gather.2
where the time goes:
time: 222 us
  blocking collectives  119 us (54%)
  waiting for transfers between devices  53.9 us (24%)
  other arithmetic  20.7 us (9%)
  between operations  15.5 us (7%)
  local copies, waits for them, and re-layouts  8.93 us (4%)
  matrix products  3.81 us (2%)
    all_gather x2, blocking collectives, merged(): everything = jax.tree.map(lambda part: lax.all_gather(part, axis), array)  61.6 us
    psum x1, blocking collectives, body(): kv_full = lax.psum(partial_kv, 'tp').astype(jnp.bfloat16)  56.9 us
    all_gather x1, waiting for transfers between devices, body(): blocks = lax.all_gather(sent, 'grp', axis=0, tiled=True)  40.8 us
    add x15, other arithmetic, combine(): mixed = blended_first * scale_a[..., None] + mixed_b * scale_b[..., None]  16.1 us
    all_gather x1, waiting for transfers between devices, merged(): everything = jax.tree.map(lambda part: lax.all_gather(part, axis), array)  13.1 us
  transfers between devices with their start and end apart: 2, of which 2 were waited for; matrix products, arithmetic and copies ran while one was open for 9% of the time, Pallas kernels for 0%

commit v1 on v0

--- a/solution.py
+++ b/solution.py
@@ -7,6 +7,7 @@
 HD = 128
 BLK = 128
 NEG = -1e30
+make_circles = lambda sheet: jnp.sum(lax.all_gather(sheet, "tp"), axis=0)
 
 
 def merged(array, axis, combine):
@@ -109,7 +110,7 @@
     ranks = lax.axis_size("tp")
     rank = lax.axis_index("tp")
     columns = kvw // ranks
-    kv_full = lax.psum(partial_kv, "tp").astype(jnp.bfloat16)
+    kv_full = make_circles(partial_kv).astype(jnp.bfloat16)
     kv_own = lax.dynamic_slice_in_dim(kv_full, rank * columns, columns, 1)
     new_kv = kv_own.reshape(steps, local_rows, columns)
     span = stored_attention_memory.shape[1]

time: 222 us -> 199 us (0.90)
  blocking collectives: 119 us -> 95.1 us
    psum x1 -> x0, blocking collectives: 56.9 us -> none  [body(): kv_full = lax.psum(partial_kv, 'tp').astype(jnp.bfloat16)]
    all_gather x0 -> x1, blocking collectives: none -> 33.5 us  [make_circles = lambda sheet: jnp.sum(lax.all_gather(sheet, 'tp'), axis=0)]
  transfers between devices with their start and end apart: 2 -> 2, of which waited for: 2 -> 2; matrix products, arithmetic and copies ran while one was open for 9% -> 10% of each run, Pallas kernels for 0% -> 0%
where the time goes in v1:
time: 199 us
  blocking collectives  95.1 us (48%)
  waiting for transfers between devices  53.9 us (27%)
  other arithmetic  20.8 us (10%)
  between operations  15.5 us (8%)
  local copies, waits for them, and re-layouts  8.94 us (4%)
  matrix products  3.81 us (2%)
    all_gather x2, blocking collectives, merged(): everything = jax.tree.map(lambda part: lax.all_gather(part, axis), array)  61.6 us
    all_gather x1, waiting for transfers between devices, body(): blocks = lax.all_gather(sent, 'grp', axis=0, tiled=True)  40.8 us
    all_gather x1, blocking collectives, make_circles = lambda sheet: jnp.sum(lax.all_gather(sheet, 'tp'), axis=0)  33.5 us
    add x15, other arithmetic, combine(): mixed = blended_first * scale_a[..., None] + mixed_b * scale_b[..., None]  16.1 us
    all_gather x1, waiting for transfers between devices, merged(): everything = jax.tree.map(lambda part: lax.all_gather(part, axis), array)  13.1 us
  transfers between devices with their start and end apart: 2, of which 2 were waited for; matrix products, arithmetic and copies ran while one was open for 10% of the time, Pallas kernels for 0%

profile of v1, /device:TPU:2, one launch (start us, length us, event | category | flops | bytes accessed | tf_op | source)
XLA Modules:
  0.0 198.7 jit_solution(14276287727001649753)
XLA Ops:
  7.2 0.0 copy-start
  7.2 0.0 all-gather.7.cloned.1.call-start
  7.2 0.0 copy-start.4
  7.2 2.9 %copy.88 = bf16[1,512,2048]{1,2,0:T(8,128)(2,1)S(1)} copy(bf16[1,512,2048]{2,1,0:T(8,128)(2,1)} %param.18) | data formatting | bytes 4194304 | tf_op args[7]
  10.8 0.0 copy-done.4
  10.8 0.0 copy-start.5
  10.8 0.0 copy-start.2
  10.8 0.0 copy-start.3
  10.9 0.4 fusion.34
  11.2 1.1 convolution_bitcast_fusion.1
  12.4 0.7 copy.130
  13.0 0.0 all-gather.7.cloned.1.call-update
  13.1 0.0 all-gather.5.cloned.1.call-start
  13.8 0.0 copy-done.5
  13.8 0.1 and_reduce_fusion
  13.9 0.0 copy-done.2
  13.9 0.0 copy-done.3
  13.9 0.7 convert_select_fusion
  14.6 0.0 all-gather.5.cloned.1.call-update
  14.6 0.7 convert_subtract_fusion
  15.3 0.2 fusion.13
  15.6 0.1 all_gather_reshape.9
  15.7 35.6 %all_gather.21 = f32[16,4,1,64]{3,1,2,0:T(4,128)S(1)} all-gather(f32[1,4,1,64]{3,1,2,0:T(4,128)S(1)} %all_gather_reshape.9), channel_id=1, replica_groups=mesh['grp'=32,'tp'=16] {'tp'}, dimensions={0}, use_global_device_ids=true | all-gather | bytes 17408 | tf_op jit(solution)/shard_map/all_gather | solution.py:14
  51.3 0.1 all_gather_reshape.10
  51.4 26.1 %all_gather.22 = f32[16,4,1,64]{3,1,2,0:T(4,128)S(1)} all-gather(f32[1,4,1,64]{3,1,2,0:T(4,128)S(1)} %all_gather_reshape.10), channel_id=1, replica_groups=mesh['grp'=32,'tp'=16] {'tp'}, dimensions={0}, use_global_device_ids=true | all-gather | bytes 17408 | tf_op jit(solution)/shard_map/all_gather | solution.py:14
  77.5 13.1 %all-gather.7.cloned.1.call-done = f32[16,4,1,64,128]{4,3,2,1,0:T(8,128)} async-done(((f32[1,4,1,64,128]{4,3,2,1,0:T(8,128)}), f32[16,4,1,64,128]{4,3,2,1,0:T(8,128)}) %all-gather.7.cloned.1.call-update) | async-done | bytes 2097168 | tf_op jit(solution)/shard_map/all_gather | solution.py:14
  90.5 0.9 slice_bitcast_fusion.4
  91.5 17.1 %while.19 = (s32[]{:T(128)}, f32[4,1,64]{2,1,0:T(1,128)S(1)}, f32[4,1,64]{2,1,0:T(1,128)S(1)}, f32[4,1,64,128]{3,2,1,0:T(8,128)S(1)}, f32[16,4,1,64]{3,1,2,0:T(4...) while((s32[]{:T(128)}, f32[4,1,64]{2,1,0:T(1,128)S(1)}, ...), condition=%wide.region_5.6_spmd, body=%wide.region_4.5_spmd.sunk | while | flops 99845 | bytes 407703 | solution.py:20
  91.5 1.1 fusion.37
  92.7 1.1 fusion.37
  93.8 1.1 fusion.37
  94.9 1.1 fusion.37
  96.1 1.1 fusion.37
  97.2 1.1 fusion.37
  98.4 1.1 fusion.37
  99.5 1.1 fusion.37
  100.6 1.1 fusion.37
  101.8 1.1 fusion.37
  102.9 1.1 fusion.37
  104.1 1.1 fusion.37
  105.2 1.1 fusion.37
  106.3 1.1 fusion.37
  107.5 1.1 fusion.37
  108.6 0.1 copy.100
  108.7 40.8 %all-gather.5.cloned.1.call-done = bf16[64,128,128]{2,1,0:T(8,128)(2,1)} async-done(((bf16[2,128,128]{2,1,0:T(8,128)(2,1)}), bf16[64,128,128]{2,1,0:T(8,128)(2,1)}) %all-gather.5.cloned.1.call-update) | async-done | bytes 2097168 | tf_op jit(solution)/shard_map/all_gather | solution.py:94
  149.5 2.1 %convert_bitcast_fusion = f32[4,128,16,128]{3,1,2,0:T(8,128)S(1)} fusion(bf16[4,16,128,128]{3,2,1,0:T(8,128)(2,1)} %bitcast.169), kind=kLoop, calls=%fused_computation.10 | loop fusion | flops 1048576 | bytes 6291456 | tf_op jit(solution)/shard_map/convert_element_type | solution.py:101
  151.6 0.0 copy-start.1
  151.6 2.4 %copy.87 = f32[4,128,16,128]{3,2,1,0:T(8,128)S(1)} copy(f32[4,128,16,128]{3,1,2,0:T(8,128)S(1)} %convert_bitcast_fusion) | data formatting | bytes 8388608 | tf_op jit(solution)/shard_map/convert_element_type | solution.py:101
  154.0 0.0 copy-done
  154.1 1.3 convolution_bitcast_fusion
  155.4 33.5 %all-gather.1 = f32[16,4,2048]{2,1,0:T(4,128)S(1)} all-gather(f32[1,4,2048]{2,1,0:T(4,128)S(1)} %convolution_bitcast_fusion), channel_id=2, replica_groups=mesh['grp'=32,'tp'=16] {'tp'}, dimensions={0}, use_global_device_ids=true | all-gather | bytes 557056 | tf_op jit(solution)/shard_map/all_gather | solution.py:10
  188.9 0.1 reduce_sum.29
  189.0 0.6 fusion.29
  189.5 0.6 gather_fusion
  190.1 0.1 bitcast_select_fusion
  190.2 0.1 fusion.35
  190.3 0.1 copy.103
  190.4 0.1 fusion.27
  190.5 0.1 copy.105
  190.6 0.1 copy.109
  190.7 0.1 fusion.31
  190.8 0.1 copy.110
  190.9 0.1 copy.104
  191.0 0.8 fusion.10
  (42 shorter events, 0.6 us)
Async XLA Ops:
  7.2 146.9 %copy-start = (bf16[4,1,512]{2,0,1:T(4,128)(2,1)S(1)}, bf16[4,1,512]{2,0,1:T(4,128)(2,1)}, u32[]{:S(2)}) copy-start(bf16[4,1,512]{2,0,1:T(4,128)(2,1)} %param.16) | copy-start | bytes 12292
  7.2 83.4 %all-gather.7.cloned.1.call-start = ((), (), s32[]{:S(2)}) async-start(), calls=%async_computation.1 | async-start | bytes 2228224 | tf_op jit(solution)/shard_map/all_gather | solution.py:14
  7.2 3.6 %copy-start.4 = (bf16[4,1,8192]{2,0,1:T(4,128)(2,1)S(1)}, bf16[4,1,8192]{2,0,1:T(4,128)(2,1)}, u32[]{:S(2)}) copy-start(bf16[4,1,8192]{2,0,1:T(4,128)(2,1)} %param.17) | copy-start | bytes 196612
  10.8 3.0 %copy-start.5 = (s32[1,2]{1,0:T(1,128)S(1)}, s32[1,2]{1,0:T(1,128)}, u32[]{:S(2)}) copy-start(s32[1,2]{1,0:T(1,128)} %param.13) | copy-start | bytes 28
  10.8 3.0 %copy-start.2 = (f32[2,128,128]{2,1,0:T(8,128)S(1)}, f32[2,128,128]{2,1,0:T(8,128)}, u32[]{:S(2)}) copy-start(f32[2,128,128]{2,1,0:T(8,128)} %param.11) | copy-start | bytes 393220
  10.8 3.0 %copy-start.3 = (f32[2,128,128]{2,1,0:T(8,128)S(1)}, f32[2,128,128]{2,1,0:T(8,128)}, u32[]{:S(2)}) copy-start(f32[2,128,128]{2,1,0:T(8,128)} %param.12) | copy-start | bytes 393220
  13.1 136.4 %all-gather.5.cloned.1.call-start = ((), (), s32[]{:S(2)}) async-start(), calls=%async_computation | async-start | bytes 2162688 | tf_op jit(solution)/shard_map/all_gather | solution.py:94
  151.6 2.5 %copy-start.1 = (bf16[512,2048]{1,0:T(8,128)(2,1)S(1)}, bf16[512,2048]{1,0:T(8,128)(2,1)}, u32[]{:S(2)}) copy-start(bf16[512,2048]{1,0:T(8,128)(2,1)} %param.15) | copy-start | bytes 6291460
Sparse Core Ops, SparseCore 0:
  13.2 77.3 all-gather.6
  93.7 55.7 all-gather.4
